TPU v7x, 128 devices: a whole 4x4x4 slice. The times are simulated.
128 devices in a mesh: prow: 16 (over x, z_hi, core), pcol: 8 (over z_lo, y).
Axes of the slice: x: 4, y: 4, z: 4 (z_hi: 2, z_lo: 2; z = z_hi * 2 + z_lo), core: 2. Of those that a mesh axis runs over, the one named last changes fastest.
Arguments:
- inverse: bfloat16 [4, 8192, 8, 4096], P(None, 'prow', None, 'pcol'), may hold values from -6 to 6
- panel: bfloat16 [2, 4, 8192, 256], P(None, None, 'prow'), may hold values from -0.0625 to 0.0625
- structure: int32 [2, 16], replicated, may hold values from 0 to 63, as said below
- diag_inverse: float32 [2, 256, 256], replicated, may hold values from -6 to 6
Outputs:
- off_diag: bfloat16 [2, 4, 8192, 256], P(None, None, ('prow', 'pcol'))
- diag_block: float32 [2, 256, 256], replicated
Inputs may be any that keep to these rules, and one draw needn't show every extreme that they name: `structure`: each row lists 16 distinct block indices in increasing order, exactly one of them congruent to p modulo 16 for every p, and always includes the last ancestor block 63.
All inputs are finite; a program needn't handle non-finite values.
Results may differ from a plain program's by a relative error of at most 0.0022.
Values may be sent and summed in bfloat16 or wider, within the bound.
No kernel may reach another device: no remote copies, remote signals or barrier semaphores. Data moves between devices by JAX's collectives and lax.ppermute only.
A program may use at most 128 MiB of HBM per device.

v0:
```python
import jax
import jax.numpy as jnp
from jax import lax
from jax.sharding import PartitionSpec as P


def cut_along(array, dim, count):
    before, after = (array.shape[:dim], array.shape[dim + 1 :])
    return jnp.moveaxis(array.reshape(*before, count, -1, *after), dim, 0)


def sum_at_owner(array, axis, dim):
    tiles = cut_along(array, dim, lax.axis_size(axis))
    arrived = lax.all_to_all(tiles, axis, split_axis=0, concat_axis=0, tiled=True)
    return arrived.sum(axis=0)


def on_device(inverse, panel, structure, diag_inverse):
    prow_count = lax.axis_size("prow")
    pcol_count = lax.axis_size("pcol")
    prow_index = lax.axis_index("prow")
    pcol_index = lax.axis_index("pcol")
    rows_local, block_size, cols_local, _ = inverse.shape
    panel_width = panel.shape[3]
    total_blocks = rows_local * prow_count
    piece_rows = block_size // pcol_count
    owner_ratio = prow_count // pcol_count
    repeat_count = cols_local // owner_ratio
    positions = jnp.arange(total_blocks, dtype=jnp.int32)
    local_rows = jnp.arange(rows_local, dtype=jnp.int32)
    pieces = []
    products = []
    for supernode in range(structure.shape[0]):
        chosen = structure[supernode]
        selected = jnp.any(chosen[:, None] == positions[None, :], axis=0)
        own_rows = lax.dynamic_index_in_dim(
            selected.reshape(rows_local, prow_count), prow_index, 1, keepdims=False
        )
        own_cols = lax.dynamic_index_in_dim(
            selected.reshape(cols_local, pcol_count), pcol_index, 1, keepdims=False
        )
        local_panel = panel[supernode]
        row_pick = jnp.sum(jnp.where(own_rows, local_rows, 0))
        single = lax.dynamic_index_in_dim(local_panel, row_pick, 0, keepdims=False)
        gathered = lax.all_gather(single, "prow", axis=0, tiled=True)
        gathered = gathered.reshape(owner_ratio, pcol_count, block_size, panel_width)
        owner_blocks = lax.dynamic_index_in_dim(gathered, pcol_index, 1, keepdims=False)
        tiled = jnp.broadcast_to(
            owner_blocks[None], (repeat_count, owner_ratio, block_size, panel_width)
        )
        tiled = tiled.reshape(cols_local, block_size, panel_width)
        column_panel = tiled * own_cols.astype(jnp.bfloat16)[:, None, None]
        ranking = jnp.where(own_cols, 0, cols_local) + jnp.arange(cols_local, dtype=jnp.int32)
        column_order = jnp.argsort(ranking)
        live_count = jnp.sum(own_cols.astype(jnp.int32))

        def add_column(position_index, running):
            column = column_order[position_index]
            block_column = lax.dynamic_index_in_dim(inverse, column, 2, keepdims=False)
            factor = lax.dynamic_index_in_dim(column_panel, column, 0, keepdims=False)
            return running + jnp.einsum(
                "rab,bw->raw", block_column, factor, preferred_element_type=jnp.float32
            )

        starting = jnp.zeros((rows_local, block_size, panel_width), jnp.float32)
        partial_value = lax.fori_loop(0, live_count, add_column, starting)
        partial_value = -partial_value * own_rows.astype(jnp.float32)[:, None, None]
        summed = sum_at_owner(partial_value, "pcol", 1)
        rounded = summed.astype(jnp.bfloat16)
        pieces.append(rounded)
        factor_rows = lax.dynamic_slice_in_dim(local_panel, pcol_index * piece_rows, piece_rows, 1)
        products.append(
            jnp.einsum("raw,rav->wv", factor_rows, rounded, preferred_element_type=jnp.float32)
        )
    diagonal_terms = lax.psum(jnp.stack(products), ("prow", "pcol"))
    return (jnp.stack(pieces), diag_inverse - diagonal_terms)


def solution(mesh):
    placed = (P(None, "prow", None, "pcol"), P(None, None, "prow", None), P(), P())
    return jax.shard_map(
        on_device,
        mesh=mesh,
        in_specs=placed,
        out_specs=(P(None, None, ("prow", "pcol"), None), P()),
        check_vma=False,
    )
```

profile of v0, /device:TPU:1, one launch (start us, length us, event | category | flops | bytes accessed | tf_op | source)
XLA Modules:
  0.0 347.8 jit_solution(9517647593599522379)
XLA Ops:
  10.6 1.7 fusion.30
  16.7 16.7 %copy.16 = bf16[4,512,8,512]{3,1,0,2:T(8,128)(2,1)} copy(bf16[4,512,8,512]{3,2,1,0:T(8,128)(2,1)} %param.8) | data formatting | bytes 33554432 | tf_op jit(solution)/shard_map/while | solution.py:66
  36.1 37.5 %all-gather.5.cloned.1.call-done = bf16[1,1,8192,256]{3,2,1,0:T(8,128)(2,1)} async-done(((bf16[1,1,512,256]{3,2,1,0:T(8,128)(2,1)}), bf16[1,1,8192,256]{3,2,1,0:T(8,128)(2,1)}) %all-gather.5.cloned.1.call-update) | async-done | bytes 4194320 | tf_op jit(solution)/shard_map/all_gather | solution.py:45
  73.6 1.1 dynamic-slice_bitcast_fusion.1
  74.7 1.6 bitcast_multiply_fusion.1
  76.4 11.7 %while.20 = (s32[]{:T(128)}, f32[4,512,256]{2,1,0:T(8,128)S(1)}, s32[]{:T(128)}, s32[8]{0:T(128)S(1)}, bf16[4,512,8,512]{3,1,0,2:T(8,128)(2,1)}, /*index=5*/bf16...) while((s32[]{:T(128)}, f32[4,512,256]{2,1,0:T(8,128)S(1)}, s32[]{:T(128)}, s32[8]{0:T(128)S(1)}, ...), condition=%wide.region_5.6_spmd, body=%wide.region_4.5_spmd.sunk | while | flops 537395200 | bytes 6554797 | solution.py:66
  79.6 2.3 fusion.41
  85.1 2.4 fusion.41
  88.4 1.5 copy.17
  89.9 4.3 %all-to-all-start = ((f32[8,4,64,256]{3,2,1,0:T(8,128)}), f32[8,4,64,256]{3,2,1,0:T(8,128)}, u32[]{:S(2)}, u32[]{:S(2)}) async-start(f32[8,4,64,256]{3,2,1,0:T(8,128)} %copy.17), calls=%async_computation | async-start | bytes 4194304 | tf_op jit(solution)/shard_map/all_to_all | solution.py:14
  95.5 45.2 %all-gather.7.cloned.1.call-done = bf16[1,1,8192,256]{3,2,1,0:T(8,128)(2,1)} async-done(((bf16[1,1,512,256]{3,2,1,0:T(8,128)(2,1)}), bf16[1,1,8192,256]{3,2,1,0:T(8,128)(2,1)}) %all-gather.7.cloned.1.call-update) | async-done | bytes 4194320 | tf_op jit(solution)/shard_map/all_gather | solution.py:45
  140.7 1.1 dynamic-slice_bitcast_fusion
  141.7 1.6 bitcast_multiply_fusion
  143.5 11.8 %while.21 = (s32[]{:T(128)}, f32[4,512,256]{2,1,0:T(8,128)S(1)}, s32[]{:T(128)}, s32[8]{0:T(128)S(1)}, bf16[4,512,8,512]{3,1,0,2:T(8,128)(2,1)}, /*index=5*/bf16...) while((s32[]{:T(128)}, f32[4,512,256]{2,1,0:T(8,128)S(1)}, s32[]{:T(128)}, s32[8]{0:T(128)S(1)}, ...), condition=%wide.region_12.13_spmd, body=%wide.region_11.12_spmd.sunk | while | flops 537395200 | bytes 6554797 | solution.py:66
  146.7 2.3 fusion.44
  152.3 2.3 fusion.44
  155.6 1.5 copy.19
  157.1 4.3 %all-to-all-start.1 = ((f32[8,4,64,256]{3,2,1,0:T(8,128)}), f32[8,4,64,256]{3,2,1,0:T(8,128)S(1)}, u32[]{:S(2)}, u32[]{:S(2)}) async-start(f32[8,4,64,256]{3,2,1,0:T(8,128)} %copy.19), calls=%async_computation.1 | async-start | bytes 4194304 | tf_op jit(solution)/shard_map/all_to_all | solution.py:14
  161.4 1.7 reduce_sum.56
  163.1 1.8 convolution_bitcast_fusion.1
  165.0 23.5 %all-to-all-done.1 = f32[8,4,64,256]{3,2,1,0:T(8,128)S(1)} async-done(((f32[8,4,64,256]{3,2,1,0:T(8,128)}), f32[8,4,64,256]{3,2,1,0:T(8,128)S(1)}, u32[]{:S(2)}, u32[]{:S(2)}) %all-to-all-start.1) | async-done | bytes 2097184 | tf_op jit(solution)/shard_map/all_to_all | solution.py:14
  188.8 1.8 pad_maximum_fusion
  191.4 148.0 %all-reduce.2.cloned.1.call-done = f32[2,256,256]{2,1,0:T(8,128)} async-done(((f32[2,256,256]{2,1,0:T(8,128)}), f32[2,256,256]{2,1,0:T(8,128)}) %all-reduce.2.cloned.1.call-update) | async-done | bytes 524304 | tf_op jit(solution)/shard_map/psum | solution.py:75
  339.4 1.9 sub.3
  (46 shorter events, 12.2 us)
Async XLA Ops:
  7.2 66.4 %all-gather.5.cloned.1.call-start = ((), (), s32[]{:S(2)}) async-start(), calls=%async_computation.3 | async-start | bytes 4456448 | tf_op jit(solution)/shard_map/all_gather | solution.py:45
  12.3 21.0 %copy-start = (bf16[1,4,512,256]{3,2,1,0:T(8,128)(2,1)}, bf16[1,4,512,256]{3,2,1,0:T(8,128)(2,1)S(1)}, u32[]{:S(2)}) copy-start(bf16[1,4,512,256]{3,2,1,0:T(8,128)(2,1)S(1)} %get-tuple-element.162) | copy-start | bytes 3145732
  13.7 126.9 %all-gather.7.cloned.1.call-start = ((), (), s32[]{:S(2)}) async-start(), calls=%async_computation.4 | async-start | bytes 4456448 | tf_op jit(solution)/shard_map/all_gather | solution.py:45
  89.9 67.2 %all-to-all-start = ((f32[8,4,64,256]{3,2,1,0:T(8,128)}), f32[8,4,64,256]{3,2,1,0:T(8,128)}, u32[]{:S(2)}, u32[]{:S(2)}) async-start(f32[8,4,64,256]{3,2,1,0:T(8,128)} %copy.17), calls=%async_computation | async-start | bytes 4194304 | tf_op jit(solution)/shard_map/all_to_all | solution.py:14
  157.1 31.4 %all-to-all-start.1 = ((f32[8,4,64,256]{3,2,1,0:T(8,128)}), f32[8,4,64,256]{3,2,1,0:T(8,128)S(1)}, u32[]{:S(2)}, u32[]{:S(2)}) async-start(f32[8,4,64,256]{3,2,1,0:T(8,128)} %copy.19), calls=%async_computation.1 | async-start | bytes 4194304 | tf_op jit(solution)/shard_map/all_to_all | solution.py:14
  161.4 178.0 %all-reduce.2.cloned.1.call-start = ((), (), s32[]{:S(2)}) async-start(), calls=%async_computation.2 | async-start | bytes 1048576 | tf_op jit(solution)/shard_map/psum | solution.py:75
  188.6 150.8 %copy-start.1 = (f32[2,256,256]{2,1,0:T(8,128)S(1)}, f32[2,256,256]{2,1,0:T(8,128)}, u32[]{:S(2)}) copy-start(f32[2,256,256]{2,1,0:T(8,128)} %param.11) | copy-start | bytes 1572868
Sparse Core Ops, SparseCore 0:
  13.9 59.6 all-gather.4
  76.6 64.0 all-gather.6
  190.8 148.5 all-reduce.1
where the time goes:
time: 349 us; the launch traced here: 348 us
  waiting for transfers between devices  254 us (73%)
  local copies, waits for them, and re-layouts  29.1 us (8%)
  between operations  17.8 us (5%)
  other arithmetic  14.8 us (4%)
  loops' own time  11.8 us (3%)
  matrix products  11.4 us (3%)
  starting transfers between devices  8.73 us (3%)
    psum x1, waiting for transfers between devices, on_device(): diagonal_terms = lax.psum(jnp.stack(products), ('prow', 'pcol'))  148 us
    all_gather x2, waiting for transfers between devices, on_device(): gathered = lax.all_gather(single, 'prow', axis=0, tiled=True)  82.7 us
    all_to_all x2, waiting for transfers between devices, sum_at_owner(): lax.all_to_all(tiles, axis, split_axis=0, concat_axis=0, tiled=True)  23.5 us
    while x1, local copies, waits for them, and re-layouts, on_device(): partial_value = lax.fori_loop(0, live_count, add_column, starting)  16.7 us
    another operation x2, loops' own time, on_device(): partial_value = lax.fori_loop(0, live_count, add_column, starting)  11.8 us
    dot_general x4, matrix products, add_column(): jnp.einsum('rab,bw->raw', block_column, factor, preferred_element_type=jn...  9.32 us
    all_to_all x2, starting transfers between devices, sum_at_owner(): lax.all_to_all(tiles, axis, split_axis=0, concat_axis=0, tiled=True)  8.61 us
  transfers between devices with their start and end apart: 5, of which 4 were waited for; matrix products, arithmetic and copies ran while one was open for 13% of the time, Pallas kernels for 0%

commit v1 on v0

--- a/solution.py
+++ b/solution.py
@@ -72,7 +72,7 @@
         products.append(
             jnp.einsum("raw,rav->wv", factor_rows, rounded, preferred_element_type=jnp.float32)
         )
-    diagonal_terms = lax.psum(jnp.stack(products), ("prow", "pcol"))
+    diagonal_terms = jnp.sum(lax.all_gather(jnp.stack(products), ("prow", "pcol")), axis=0)
     return (jnp.stack(pieces), diag_inverse - diagonal_terms)
 
 

time: 349 us -> 613 us (1.76)
  waiting for transfers between devices: 254 us -> 498 us
  other arithmetic: 14.8 us -> 34.7 us
    all_gather x0 -> x1, waiting for transfers between devices: none -> 392 us  [on_device(): lax.all_gather(jnp.stack(products), ('prow', 'pcol'))]
    psum x1 -> x0, waiting for transfers between devices: 148 us -> none  [on_device(): diagonal_terms = lax.psum(jnp.stack(products), ('prow', 'pcol'))]
    reduce_sum x0 -> x1, other arithmetic: none -> 20.9 us  [on_device(): jnp.sum(lax.all_gather(jnp.stack(products), ('prow', 'pcol')), axis=0)]
  transfers between devices with their start and end apart: 5 -> 5, of which waited for: 4 -> 4; matrix products, arithmetic and copies ran while one was open for 13% -> 8% of each run, Pallas kernels for 0% -> 0%
where the time goes in v1:
time: 613 us; the launch traced here: 612 us
  waiting for transfers between devices  498 us (81%)
  other arithmetic  34.7 us (6%)
  local copies, waits for them, and re-layouts  29.1 us (5%)
  between operations  17.8 us (3%)
  loops' own time  11.8 us (2%)
  matrix products  11.4 us (2%)
  starting transfers between devices  8.73 us (1%)
    all_gather x1, waiting for transfers between devices, on_device(): lax.all_gather(jnp.stack(products), ('prow', 'pcol'))  392 us
    all_gather x2, waiting for transfers between devices, on_device(): gathered = lax.all_gather(single, 'prow', axis=0, tiled=True)  82.7 us
    all_to_all x2, waiting for transfers between devices, sum_at_owner(): lax.all_to_all(tiles, axis, split_axis=0, concat_axis=0, tiled=True)  23.5 us
    reduce_sum x1, other arithmetic, on_device(): jnp.sum(lax.all_gather(jnp.stack(products), ('prow', 'pcol')), axis=0)  20.9 us
    while x1, local copies, waits for them, and re-layouts, on_device(): partial_value = lax.fori_loop(0, live_count, add_column, starting)  16.7 us
  transfers between devices with their start and end apart: 5, of which 4 were waited for; matrix products, arithmetic and copies ran while one was open for 8% of the time, Pallas kernels for 0%

profile of v1, /device:TPU:1, one launch (start us, length us, event | category | flops | bytes accessed | tf_op | source)
XLA Modules:
  0.0 611.9 jit_solution(17691803305578428339)
XLA Ops:
  10.6 1.7 fusion.30
  16.7 16.7 %copy.16 = bf16[4,512,8,512]{3,1,0,2:T(8,128)(2,1)} copy(bf16[4,512,8,512]{3,2,1,0:T(8,128)(2,1)} %param.8) | data formatting | bytes 33554432 | tf_op jit(solution)/shard_map/while | solution.py:66
  36.1 37.5 %all-gather.7.cloned.1.call-done = bf16[1,1,8192,256]{3,2,1,0:T(8,128)(2,1)} async-done(((bf16[1,1,512,256]{3,2,1,0:T(8,128)(2,1)}), bf16[1,1,8192,256]{3,2,1,0:T(8,128)(2,1)}) %all-gather.7.cloned.1.call-update) | async-done | bytes 4194320 | tf_op jit(solution)/shard_map/all_gather | solution.py:45
  73.6 1.1 dynamic-slice_bitcast_fusion.1
  74.7 1.6 bitcast_multiply_fusion.1
  76.4 11.7 %while.20 = (s32[]{:T(128)}, f32[4,512,256]{2,1,0:T(8,128)S(1)}, s32[]{:T(128)}, s32[8]{0:T(128)S(1)}, bf16[4,512,8,512]{3,1,0,2:T(8,128)(2,1)}, /*index=5*/bf16...) while((s32[]{:T(128)}, f32[4,512,256]{2,1,0:T(8,128)S(1)}, s32[]{:T(128)}, s32[8]{0:T(128)S(1)}, ...), condition=%wide.region_5.6_spmd, body=%wide.region_4.5_spmd.sunk | while | flops 537395200 | bytes 6554797 | solution.py:66
  79.6 2.3 fusion.41
  85.1 2.4 fusion.41
  88.4 1.5 copy.17
  89.9 4.3 all-to-all-start
  95.5 45.2 %all-gather.9.cloned.1.call-done = bf16[1,1,8192,256]{3,2,1,0:T(8,128)(2,1)} async-done(((bf16[1,1,512,256]{3,2,1,0:T(8,128)(2,1)}), bf16[1,1,8192,256]{3,2,1,0:T(8,128)(2,1)}) %all-gather.9.cloned.1.call-update) | async-done | bytes 4194320 | tf_op jit(solution)/shard_map/all_gather | solution.py:45
  140.7 1.1 dynamic-slice_bitcast_fusion
  141.7 1.6 bitcast_multiply_fusion
  143.5 11.8 %while.21 = (s32[]{:T(128)}, f32[4,512,256]{2,1,0:T(8,128)S(1)}, s32[]{:T(128)}, s32[8]{0:T(128)S(1)}, bf16[4,512,8,512]{3,1,0,2:T(8,128)(2,1)}, /*index=5*/bf16...) while((s32[]{:T(128)}, f32[4,512,256]{2,1,0:T(8,128)S(1)}, s32[]{:T(128)}, s32[8]{0:T(128)S(1)}, ...), condition=%wide.region_12.13_spmd, body=%wide.region_11.12_spmd.sunk | while | flops 537395200 | bytes 6554797 | solution.py:66
  146.7 2.3 fusion.44
  152.3 2.3 fusion.44
  155.6 1.5 copy.19
  157.1 4.3 all-to-all-start.1
  161.4 1.7 reduce_sum.65
  163.1 1.8 convolution_bitcast_fusion.1
  165.0 23.5 %all-to-all-done.1 = f32[8,4,64,256]{3,2,1,0:T(8,128)S(1)} async-done(((f32[8,4,64,256]{3,2,1,0:T(8,128)}), f32[8,4,64,256]{3,2,1,0:T(8,128)S(1)}, u32[]{:S(2)}, u32[]{:S(2)}) %all-to-all-start.1) | async-done | bytes 2097184 | tf_op jit(solution)/shard_map/all_to_all | solution.py:14
  188.8 1.8 pad_maximum_fusion
  191.4 392.2 %all-gather.11.cloned.1.call-done = f32[256,256,256]{2,1,0:T(8,128)} async-done(((f32[2,256,256]{2,1,0:T(8,128)}), f32[256,256,256]{2,1,0:T(8,128)}) %all-gather.11.cloned.1.call-update) | async-done | bytes 67108880 | tf_op jit(solution)/shard_map/all_gather | solution.py:75
  583.6 20.9 %reduce_sum.69 = f32[2,256,256]{2,1,0:T(8,128)S(1)} reduce(f32[128,2,256,256]{3,2,1,0:T(8,128)} %bitcast.28, f32[]{:T(128)} %constant.66.clone.1), dimensions={0}, to_apply=%region_14.15 | reduce | flops 16646144 | bytes 67633152 | tf_op jit(solution)/shard_map/reduce_sum | solution.py:75
  (47 shorter events, 13.1 us)
Async XLA Ops:
  7.2 66.4 %all-gather.7.cloned.1.call-start = ((), (), s32[]{:S(2)}) async-start(), calls=%async_computation.2 | async-start | bytes 4456448 | tf_op jit(solution)/shard_map/all_gather | solution.py:45
  12.3 21.0 %copy-start = (bf16[1,4,512,256]{3,2,1,0:T(8,128)(2,1)}, bf16[1,4,512,256]{3,2,1,0:T(8,128)(2,1)S(1)}, u32[]{:S(2)}) copy-start(bf16[1,4,512,256]{3,2,1,0:T(8,128)(2,1)S(1)} %get-tuple-element.162) | copy-start | bytes 3145732
  13.7 126.9 %all-gather.9.cloned.1.call-start = ((), (), s32[]{:S(2)}) async-start(), calls=%async_computation.3 | async-start | bytes 4456448 | tf_op jit(solution)/shard_map/all_gather | solution.py:45
  89.9 67.2 %all-to-all-start = ((f32[8,4,64,256]{3,2,1,0:T(8,128)}), f32[8,4,64,256]{3,2,1,0:T(8,128)}, u32[]{:S(2)}, u32[]{:S(2)}) async-start(f32[8,4,64,256]{3,2,1,0:T(8,128)} %copy.17), calls=%async_computation | async-start | bytes 4194304 | tf_op jit(solution)/shard_map/all_to_all | solution.py:14
  157.1 31.4 %all-to-all-start.1 = ((f32[8,4,64,256]{3,2,1,0:T(8,128)}), f32[8,4,64,256]{3,2,1,0:T(8,128)S(1)}, u32[]{:S(2)}, u32[]{:S(2)}) async-start(f32[8,4,64,256]{3,2,1,0:T(8,128)} %copy.19), calls=%async_computation.1 | async-start | bytes 4194304 | tf_op jit(solution)/shard_map/all_to_all | solution.py:14
  161.4 422.2 %all-gather.11.cloned.1.call-start = ((), (), s32[]{:S(2)}) async-start(), calls=%async_computation.4 | async-start | bytes 67633152 | tf_op jit(solution)/shard_map/all_gather | solution.py:75
  583.6 20.9 %copy-start.1 = (f32[2,256,256]{2,1,0:T(8,128)S(1)}, f32[2,256,256]{2,1,0:T(8,128)}, u32[]{:S(2)}) copy-start(f32[2,256,256]{2,1,0:T(8,128)} %param.11) | copy-start | bytes 1572868
Sparse Core Ops, SparseCore 0:
  13.9 59.6 all-gather.6
  76.6 64.0 all-gather.8
  190.7 392.7 all-gather.10
